TPU v7x, 128 devices: a whole 4x4x4 slice. The times are simulated.
128 devices in a mesh: vc: 8 (over x, y_hi), op: 16 (over y_lo, z, core).
Axes of the slice: x: 4, y: 4 (y_hi: 2, y_lo: 2; y = y_hi * 2 + y_lo), z: 4, core: 2. Of those that a mesh axis runs over, the one named last changes fastest.
Arguments:
- integrals: float32 [1024, 32768], P('op', 'vc'), may hold values from -0.046875 to 0.046875
- amplitudes: float32 [32768, 16384], P('vc', 'op'), may hold values from -6 to 6
- vir_energy: float32 [1024], P('vc'), may hold values from 1 to 10
- occ_energy: float32 [16384], P('op'), may hold values from -4 to -0.5
Outputs:
- update: float32 [1024, 16384], P('vc', 'op')
All inputs are finite; a program needn't handle non-finite values.
Results may differ from a plain program's by a relative error of at most 0.000076.
Values sent between devices are 32-bit elements; how exact they have to be, the bound alone decides.
A program may use at most 128 MiB of HBM per device.

v0:
```python
import jax
import jax.numpy as jnp
from jax import lax
from jax.sharding import Mesh
from jax.sharding import PartitionSpec as P

VC = ("vc_0", "vc_1")


def in_order(blocks, dim):
    dims = list(blocks.shape[1:])
    dims[dim] *= blocks.shape[0]
    return jnp.moveaxis(blocks, 0, dim).reshape(dims)


def work_in_pieces(shard, axis, dim, work, out_dim):
    extent = shard.shape[dim]
    pieces = jnp.split(shard, 2, axis=dim) if extent % 2 == 0 else [shard]
    initial = jnp.arange(lax.axis_size(axis)) * extent
    blocks = [lax.all_gather(piece, axis) for piece in pieces]
    made = [jax.vmap(work)(b, initial + k * (extent // len(pieces))) for k, b in enumerate(blocks)]
    return in_order(jnp.concatenate(made, axis=out_dim + 1), out_dim)


def sum_by_axis(shard, axes, dim):
    if not axes:
        return shard
    nearer = lax.psum_scatter(shard, axes[0], scatter_dimension=dim, tiled=True)
    return sum_by_axis(nearer, axes[1:], dim)


def shards(integrals, amplitudes, vir_energy, occ_energy):

    def product(piece, start):
        return jnp.dot(
            piece, amplitudes, precision=lax.Precision.HIGHEST, preferred_element_type=jnp.float32
        )

    partial_sum = work_in_pieces(integrals, "op", 0, product, 0)
    ladder = sum_by_axis(partial_sum, VC, 0)
    return ladder / (occ_energy[None, :] - vir_energy[:, None])


def solution(mesh):
    torus = Mesh(mesh.devices.reshape(4, 2, mesh.shape["op"]), ("vc_0", "vc_1", "op"))
    return jax.shard_map(
        shards,
        mesh=torus,
        in_specs=(P("op", VC), P(VC, "op"), P(VC), P("op")),
        out_specs=P(VC, "op"),
        check_vma=False,
    )
```

profile of v0, /device:TPU:6, one launch (start us, length us, event | category | flops | bytes accessed | tf_op | source)
XLA Modules:
  0.0 234.6 jit_solution(10663395352705994566)
XLA Ops:
  6.5 0.0 all-gather.5.cloned.1.call-start
  6.5 2.3 fusion.4
  8.8 0.0 all-gather.5.cloned.1.call-update
  8.8 0.0 all-gather.7.cloned.1.call-start
  8.9 0.7 all-gather.7.cloned.1.call-update
  9.6 0.0 reduce-scatter.3.cloned.1.call-start
  9.6 54.0 %all-gather.5.cloned.1.call-done = f32[512,4096]{1,0:T(8,128)} async-done(((f32[32,4096]{1,0:T(8,128)}), f32[512,4096]{1,0:T(8,128)}) %all-gather.5.cloned.1.call-update) | async-done | bytes 8388624 | tf_op jit(solution)/shard_map/all_gather | solution.py:20
  63.6 30.7 %fusion.2 = f32[16,32,1024]{2,1,0:T(8,128)S(1)} fusion(f32[16,32,4096]{2,1,0:T(8,128)} %bitcast.11, f32[4096,1024]{1,0:T(8,128)} %param.5), kind=kOutput, calls=%fused_computation.2 | convolution fusion | flops 25769803776 | bytes 27262976 | tf_op jit(solution)/shard_map/vmap()/dot_general | solution.py:35
  94.3 24.2 %all-gather.7.cloned.1.call-done = f32[512,4096]{1,0:T(8,128)} async-done(((f32[32,4096]{1,0:T(8,128)}), f32[512,4096]{1,0:T(8,128)}) %all-gather.7.cloned.1.call-update) | async-done | bytes 8388624 | tf_op jit(solution)/shard_map/all_gather | solution.py:20
  118.4 30.7 %fusion = f32[16,32,1024]{2,1,0:T(8,128)S(1)} fusion(f32[16,32,4096]{2,1,0:T(8,128)} %bitcast.12, f32[4096,1024]{1,0:T(8,128)} %param.5), kind=kOutput, calls=%fused_computation | convolution fusion | flops 25769803776 | bytes 27262976 | tf_op jit(solution)/shard_map/vmap()/dot_general | solution.py:35
  149.1 0.0 copy-start
  149.1 0.0 copy-start.1
  149.2 2.5 %pad_maximum_fusion = f32[16,64,1024]{2,1,0:T(8,128)} fusion(f32[16,32,1024]{2,1,0:T(8,128)S(1)} %fusion, f32[16,32,1024]{2,1,0:T(8,128)S(1)} %fusion.2), kind=kLoop, calls=%fused_computation.4 | loop fusion | flops 1048576 | bytes 8388608 | tf_op jit(solution)/shard_map/concatenate | solution.py:22
  151.7 0.0 reduce-scatter.3.cloned.1.call-update
  151.7 0.0 reduce-scatter.5.cloned.1.call-start
  151.7 46.0 %reduce-scatter.3.cloned.1.call-done = f32[256,1024]{1,0:T(8,128)} async-done(((f32[1024,1024]{1,0:T(8,128)}), f32[256,1024]{1,0:T(8,128)}) %reduce-scatter.3.cloned.1.call-update) | async-done | bytes 1048592 | tf_op jit(solution)/shard_map/reduce_scatter | solution.py:28
  197.7 0.0 reduce-scatter.5.cloned.1.call-update
  197.8 28.3 %reduce-scatter.5.cloned.1.call-done = f32[128,1024]{1,0:T(8,128)} async-done(((f32[256,1024]{1,0:T(8,128)}), f32[128,1024]{1,0:T(8,128)}) %reduce-scatter.5.cloned.1.call-update) | async-done | bytes 524304 | tf_op jit(solution)/shard_map/reduce_scatter | solution.py:28
  226.0 0.0 copy-done
  226.0 0.0 copy-done.1
  226.1 2.0 subtract_divide_fusion
Async XLA Ops:
  6.5 57.0 %all-gather.5.cloned.1.call-start = ((), (), s32[]{:S(2)}) async-start(), calls=%async_computation.4 | async-start | bytes 8912896 | tf_op jit(solution)/shard_map/all_gather | solution.py:20
  8.8 109.6 %all-gather.7.cloned.1.call-start = ((), (), s32[]{:S(2)}) async-start(), calls=%async_computation.5 | async-start | bytes 8912896 | tf_op jit(solution)/shard_map/all_gather | solution.py:20
  9.6 188.2 %reduce-scatter.3.cloned.1.call-start = ((), (), s32[]{:S(2)}) async-start(), calls=%async_computation.2 | async-start | bytes 5242880 | tf_op jit(solution)/shard_map/reduce_scatter | solution.py:28
  149.1 76.9 %copy-start = (f32[1024]{0:T(1024)S(1)}, f32[1024]{0:T(1024)}, u32[]{:S(2)}) copy-start(f32[1024]{0:T(1024)} %param.7) | copy-start | bytes 12292
  149.1 76.9 %copy-start.1 = (f32[128]{0:T(128)S(1)}, f32[128]{0:T(128)}, u32[]{:S(2)}) copy-start(f32[128]{0:T(128)} %param.6) | copy-start | bytes 1540
  151.7 74.4 %reduce-scatter.5.cloned.1.call-start = ((), (), s32[]{:S(2)}) async-start(), calls=%async_computation.3 | async-start | bytes 1572864 | tf_op jit(solution)/shard_map/reduce_scatter | solution.py:28
Sparse Core Ops, SparseCore 0:
  9.1 54.4 all-gather.4
  65.3 53.1 all-gather.6
  151.8 45.8 reduce-scatter.2
  200.1 25.9 reduce-scatter.4
where the time goes:
time: 236 us; the launch traced here: 235 us
  waiting for transfers between devices  153 us (65%)
  matrix products  61.4 us (26%)
  between operations  13.2 us (6%)
  other arithmetic  4.47 us (2%)
    all_gather x2, waiting for transfers between devices, work_in_pieces(): blocks = [lax.all_gather(piece, axis) for piece in pieces]  78.1 us
    reduce_scatter x2, waiting for transfers between devices, sum_by_axis(): nearer = lax.psum_scatter(shard, axes[0], scatter_dimension=dim, tiled=True)  74.3 us
    dot_general x2, matrix products, product(): jnp.dot(piece, amplitudes, precision=lax.Precision.HIGHEST, preferred_ele...  61.4 us
  transfers between devices with their start and end apart: 4, of which 4 were waited for; matrix products, arithmetic and copies ran while one was open for 13% of the time, Pallas kernels for 0%

commit v1 on v0

v1 whole, which is shorter than its diff:
```python
import jax
import jax.numpy as jnp
from jax import lax
from jax.experimental import pallas as pl
from jax.experimental.pallas import tpu as pltpu
from jax.sharding import PartitionSpec as P

MESH = pl.DeviceIdType.MESH
PIECES = 4
DEPTH = 1024
HALF = 64
ROWS = 128
COLS = 256
NB = 4
STAGE = 512
SLOTS = 8

OWN, ACROSS = (0, 0), (1, 0)


def slot_of(place):
    return place[0] * 4 + place[1]


WAY = {
    (0, 0): 1, (0, 1): -1, (0, 2): 1, (0, 3): -1,
    (1, 0): -1, (1, 1): 1, (1, 2): 0,
}


def rows_of(place, piece):
    if place == (1, 2) and piece == 2:
        return [(0, 32), (32, 32)]
    return [(0, 64)]


GROUPS = [
    [((1, 0), 0), ((0, 1), 0), ((0, 3), 0)],
    [((1, 0), 1), ((0, 1), 1), ((0, 3), 1)],
    [((1, 0), 2), ((0, 1), 2), ((0, 3), 2)],
    [((1, 0), 3), ((0, 1), 3), ((0, 3), 3)],
    [((0, 2), 0), ((1, 1), 0), ((1, 1), 3)],
    [((1, 3), 0), ((0, 2), 1), ((1, 3), 3)],
    [((1, 3), 1), ((1, 1), 1)],
    [((0, 2), 2), ((1, 1), 2)],
    [((1, 3), 2), ((0, 2), 3)],
    [((1, 2), 1), ((1, 2), 0), ((1, 2), 3)],
    [((1, 2), 2)],
]
EARLY = [(0, 0), (1, 0), (0, 1), (0, 3)]
EARLY_AT = 9


def relays(place, piece):
    dy, dz = place
    out = []
    if place == OWN:
        return [("z+", (0, 3), 0, 64), ("z-", (0, 1), 0, 64), ("y", (1, 0), 0, 64)]
    if piece < 3:
        if place == ACROSS:
            return [("z+", (1, 3), 0, 64), ("z-", (1, 1), 0, 64)]
        if dz == 3 and WAY[dy, piece] >= 0:
            rows = (0, 32) if WAY[dy, piece] == 0 else (0, 64)
            out.append(("z+", (dy, 2), *rows))
        if dz == 1 and WAY[dy, piece] <= 0:
            rows = (32, 32) if WAY[dy, piece] == 0 else (0, 64)
            out.append(("z-", (dy, 2), *rows))
        return out
    if dy == 0:
        if dz == 1:
            out.append(("z-", (0, 2), 0, 64))
        out.append(("y", (1, dz), 0, 64))
    return out


def kernel(
    i_hbm, t_hbm, o_ref,
    got, thi, tlo, stage, part, rx, ry, sy, ihi, ilo,
    stage_sem, own_sem, send_sem, recv_sem, fwd_sem, sib_sem,
    xs_sem, xr_sem, ys_sem, yr_sem,
):
    vc, op = lax.axis_index("vc"), lax.axis_index("op")
    x, yh = vc // 2, vc % 2
    yl, z, core = op // 8, (op // 2) % 4, op % 2

    def at(x_, yh_, yl_, z_, core_):
        return {"vc": x_ * 2 + yh_, "op": yl_ * 8 + z_ * 2 + core_}

    to = {
        "z+": at(x, yh, yl, (z + 1) % 4, core),
        "z-": at(x, yh, yl, (z + 3) % 4, core),
        "y": at(x, yh, 1 - yl, z, core),
        "c": at(x, yh, yl, z, 1 - core),
    }
    opposite = at(x, 1 - yh, yl, z, core)

    def stage_copy(s):
        return pltpu.make_async_copy(
            t_hbm.at[pl.ds(s * STAGE, STAGE)], stage.at[s % 2], stage_sem.at[s % 2]
        )

    stage_copy(0).start()
    stage_copy(1).start()

    first = pl.multiple_of(core * HALF, HALF)
    mine = [
        pltpu.make_async_copy(
            i_hbm.at[:, pl.ds(p * DEPTH, DEPTH)],
            got.at[0, p, pl.ds(first, HALF)],
            own_sem.at[p],
        )
        for p in range(PIECES)
    ]
    for copy in mine:
        copy.start()

    barrier = pltpu.get_barrier_semaphore()
    partners = list(to.values()) + [opposite]
    partners += [at((x + d) % 4, yh, yl, z, core) for d in (1, 2, 3)]
    for partner in partners:
        pl.semaphore_signal(barrier, inc=1, device_id=partner, device_id_type=MESH)
    pl.semaphore_wait(barrier, len(partners))

    started = []
    counts = {"send": 0, "fwd": 0}

    def rows_at(start, size):
        return pl.ds(pl.multiple_of(first + start, 32), size)

    def send(src, link, place, piece, start, size):
        which = 1 if (start and size < HALF) else 0
        copy = pltpu.make_async_remote_copy(
            src_ref=src,
            dst_ref=got.at[slot_of(place), piece, rows_at(start, size)],
            send_sem=send_sem.at[counts["send"]],
            recv_sem=recv_sem.at[slot_of(place), piece, which],
            device_id=to[link],
            device_id_type=MESH,
        )
        counts["send"] += 1
        copy.start()
        started.append(copy)

    def forward(src, place, piece, start, size):
        which = 1 if (start and size < HALF) else 0
        copy = pltpu.make_async_remote_copy(
            src_ref=src,
            dst_ref=got.at[slot_of(place), piece, rows_at(start, size)],
            send_sem=fwd_sem.at[counts["fwd"]],
            recv_sem=sib_sem.at[slot_of(place), piece, which],
            device_id=to["c"],
            device_id_type=MESH,
        )
        counts["fwd"] += 1
        copy.start()
        started.append(copy)

    def arrived(sem, place, piece, base, start, size):
        which = 1 if (start and size < HALF) else 0
        rows = pl.ds(pl.multiple_of(base + start, 32), size)
        ref = got.at[slot_of(place), piece, rows]
        pltpu.make_async_remote_copy(
            src_ref=ref,
            dst_ref=ref,
            send_sem=send_sem.at[0],
            recv_sem=sem.at[slot_of(place), piece, which],
            device_id=to["c"],
            device_id_type=MESH,
        ).wait_recv()

    for p in range(PIECES):
        src = i_hbm.at[:, pl.ds(p * DEPTH, DEPTH)]
        for link, place, start, size in relays(OWN, p):
            send(src, link, place, p, start, size)
        forward(src, OWN, p, 0, HALF)

    def split_stage(s):
        stage_copy(s).wait()

        @pl.loop(0, STAGE // 128)
        def _(k):
            rows = pl.ds(pl.multiple_of(k * 128, 128), 128)
            into = pl.ds(pl.multiple_of(s * STAGE + k * 128, 128), 128)
            for j in range(NB):
                v = stage[s % 2, rows, j * COLS : (j + 1) * COLS]
                h = v.astype(jnp.bfloat16)
                thi[j, into, :] = h
                tlo[j, into, :] = (v - h.astype(jnp.float32)).astype(jnp.bfloat16)

        if s + 2 < 4096 // STAGE:
            stage_copy(s + 2).start()

    def block_owner(slot):
        row = (yl + slot // 4) % 2
        ring = (z + slot % 4) % 4
        return row * 2 + ring // 2, ring % 2

    def x_copy(slot, j):
        ox, oyh = block_owner(slot)
        return pltpu.make_async_remote_copy(
            src_ref=part.at[slot, j],
            dst_ref=rx.at[oyh, (x + 3 - ox) % 4, j],
            send_sem=xs_sem.at[slot, j],
            recv_sem=xr_sem.at[oyh, (x + 3 - ox) % 4, j],
            device_id=at(ox, yh, yl, z, core),
            device_id_type=MESH,
        )

    done = {}

    def unit(place, piece):
        slot = slot_of(place)
        fresh = slot not in done
        done[slot] = done.get(slot, 0) + 1
        last = done[slot] == PIECES
        a = got[slot, piece]
        h = a.astype(jnp.bfloat16)
        ihi[...] = h
        ilo[...] = (a - h.astype(jnp.float32)).astype(jnp.bfloat16)
        depth = pl.ds(piece * DEPTH, DEPTH)
        ox, _ = block_owner(slot)

        @pl.loop(0, NB)
        def _(j):
            t = thi[j, depth, :]
            r = jnp.dot(ihi[...], t, preferred_element_type=jnp.float32)
            r += jnp.dot(ilo[...], t, preferred_element_type=jnp.float32)
            r += jnp.dot(ihi[...], tlo[j, depth, :], preferred_element_type=jnp.float32)
            part[slot, j] = r if fresh else part[slot, j] + r
            if last:
                @pl.when(ox != x)
                def _():
                    x_copy(slot, j).start()

    for p in range(PIECES):
        split_stage(2 * p)
        split_stage(2 * p + 1)
        mine[p].wait()
        arrived(sib_sem, OWN, p, HALF - first, 0, HALF)
        unit(OWN, p)

    def my_slot(parity):
        row = (x // 2 + yl) % 2
        ring = (2 * (x % 2) + parity + 4 - z) % 4
        return row * 4 + ring

    def summed(parity, j):
        for k in range(3):
            pltpu.make_async_remote_copy(
                src_ref=rx.at[parity, k, j],
                dst_ref=rx.at[parity, k, j],
                send_sem=xs_sem.at[0, 0],
                recv_sem=xr_sem.at[parity, k, j],
                device_id=opposite,
                device_id_type=MESH,
            ).wait_recv()
        total = part[my_slot(parity), j]
        for k in range(3):
            total += rx[parity, k, j]
        return total

    def y_copy(j):
        return pltpu.make_async_remote_copy(
            src_ref=sy.at[j],
            dst_ref=ry.at[j],
            send_sem=ys_sem.at[j],
            recv_sem=yr_sem.at[j],
            device_id=opposite,
            device_id_type=MESH,
        )

    def pass_on():
        @pl.loop(0, NB)
        def _(j):
            sy[j] = summed(1 - yh, j)
            y_copy(j).start()

    theirs = my_slot(1 - yh)
    early = theirs == slot_of(EARLY[0])
    for place in EARLY[1:]:
        early = early | (theirs == slot_of(place))

    for number, group in enumerate(GROUPS):
        if number == EARLY_AT:
            pl.when(early)(pass_on)
        for place, piece in group:
            for start, size in rows_of(place, piece):
                arrived(recv_sem, place, piece, first, start, size)
                src = got.at[slot_of(place), piece, rows_at(start, size)]
                forward(src, place, piece, start, size)
            for link, where, start, size in relays(place, piece):
                src = got.at[slot_of(place), piece, rows_at(start, size)]
                send(src, link, where, piece, start, size)
        for place, piece in group:
            for start, size in rows_of(place, piece):
                arrived(sib_sem, place, piece, HALF - first, start, size)
            unit(place, piece)

    pl.when(jnp.logical_not(early))(pass_on)

    @pl.loop(0, NB)
    def _(j):
        total = summed(yh, j)
        y_copy(j).wait_recv()
        o_ref[:, pl.ds(pl.multiple_of(j * COLS, COLS), COLS)] = total + ry[j]

    for copy in started:
        copy.wait_send()

    @pl.loop(0, NB)
    def _(j):
        y_copy(j).wait_send()
        for slot in range(SLOTS):
            @pl.when(block_owner(slot)[0] != x)
            def _():
                x_copy(slot, j).wait_send()


def shards(integrals, amplitudes, vir_energy, occ_energy):
    f32, bf16, dma = jnp.float32, jnp.bfloat16, pltpu.SemaphoreType.DMA
    ladder = pl.pallas_call(
        kernel,
        out_shape=jax.ShapeDtypeStruct((ROWS, NB * COLS), f32),
        in_specs=[pl.BlockSpec(memory_space=pl.ANY)] * 2,
        out_specs=pl.BlockSpec(memory_space=pltpu.VMEM),
        scratch_shapes=[
            pltpu.VMEM((SLOTS, PIECES, ROWS, DEPTH), f32),
            pltpu.VMEM((NB, PIECES * DEPTH, COLS), bf16),
            pltpu.VMEM((NB, PIECES * DEPTH, COLS), bf16),
            pltpu.VMEM((2, STAGE, NB * COLS), f32),
            pltpu.VMEM((SLOTS, NB, ROWS, COLS), f32),
            pltpu.VMEM((2, 3, NB, ROWS, COLS), f32),
            pltpu.VMEM((NB, ROWS, COLS), f32),
            pltpu.VMEM((NB, ROWS, COLS), f32),
            pltpu.VMEM((ROWS, DEPTH), bf16),
            pltpu.VMEM((ROWS, DEPTH), bf16),
            dma((2,)),
            dma((PIECES,)),
            dma((40,)),
            dma((SLOTS, PIECES, 2)),
            dma((40,)),
            dma((SLOTS, PIECES, 2)),
            dma((SLOTS, NB)),
            dma((2, 3, NB)),
            dma((NB,)),
            dma((NB,)),
        ],
        compiler_params=pltpu.CompilerParams(
            collective_id=0, has_side_effects=True, vmem_limit_bytes=60 << 20
        ),
        name="ladder",
    )(integrals, amplitudes)
    return ladder / (occ_energy[None, :] - vir_energy[:, None])


def solution(mesh):
    return jax.shard_map(
        shards,
        mesh=mesh,
        in_specs=(P("op", "vc"), P("vc", "op"), P("vc"), P("op")),
        out_specs=P("vc", "op"),
        check_vma=False,
    )
```

time: 236 us -> 124 us (0.53)
  waiting for transfers between devices: 153 us -> 0 us
  Pallas kernels: 0 us -> 122 us
  matrix products: 61.4 us -> 0 us
  between operations: 13.2 us -> 0.03 us
  other arithmetic: 4.47 us -> 1.98 us
    pallas_call x0 -> x1, Pallas kernels: none -> 122 us  [shards(): pl.pallas_call(kernel, out_shape=jax.ShapeDtypeStruct((ROWS, NB * COLS),...]
    all_gather x2 -> x0, waiting for transfers between devices: 78.1 us -> none  [work_in_pieces(): blocks = [lax.all_gather(piece, axis) for piece in pieces]]
    reduce_scatter x2 -> x0, waiting for transfers between devices: 74.3 us -> none  [sum_by_axis(): nearer = lax.psum_scatter(shard, axes[0], scatter_dimension=dim, tiled=True)]
    dot_general x2 -> x0, matrix products: 61.4 us -> none  [product(): jnp.dot(piece, amplitudes, precision=lax.Precision.HIGHEST, preferred_ele...]
    concatenate x1 -> x0, other arithmetic: 2.49 us -> none  [work_in_pieces(): return in_order(jnp.concatenate(made, axis=out_dim + 1), out_dim)]
  transfers between devices with their start and end apart: 4 -> 0, of which waited for: 4 -> 0; matrix products, arithmetic and copies ran while one was open for 13% -> 0% of each run, Pallas kernels for 0% -> 0%
where the time goes in v1:
time: 124 us
  Pallas kernels  122 us (98%)
  other arithmetic  1.98 us (2%)
    pallas_call x1, Pallas kernels, shards(): pl.pallas_call(kernel, out_shape=jax.ShapeDtypeStruct((ROWS, NB * COLS),...  122 us

profile of v1, /device:TPU:6, one launch (start us, length us, event | category | flops | bytes accessed | tf_op | source)
XLA Modules:
  0.0 124.2 jit_solution(2451777407032705288)
XLA Ops:
  0.0 0.0 copy-start
  0.0 0.0 copy-start.1
  0.0 122.2 %ladder.1 = f32[128,1024]{1,0:T(8,128)} custom-call(f32[64,4096]{1,0:T(8,128)} %i_hbm.1, f32[4096,1024]{1,0:T(8,128)} %t_hbm.1), custom_call_target="tpu_custom_call" | custom-call | tf_op jit(solution)/shard_map/ladder/pallas_call | solution.py:321
  122.2 0.0 copy-done
  122.2 0.0 copy-done.1
  122.2 2.0 %subtract_divide_fusion = f32[128,1024]{1,0:T(8,128)} fusion(f32[128,1024]{1,0:T(8,128)} %ladder.1, f32[128]{0:T(128)S(1)} %copy-done.1, f32[1024]{0:T(1024)S(1)} %copy-done), kind=kLoop, calls=%fused_computation | loop fusion | flops 262144 | bytes 1053184 | tf_op jit(solution)/shard_map/div | solution.py:353
Async XLA Ops:
  0.0 122.2 %copy-start = (f32[1024]{0:T(1024)S(1)}, f32[1024]{0:T(1024)}, u32[]{:S(2)}) copy-start(f32[1024]{0:T(1024)} %param.7) | copy-start | bytes 12292
  0.0 122.2 %copy-start.1 = (f32[128]{0:T(128)S(1)}, f32[128]{0:T(128)}, u32[]{:S(2)}) copy-start(f32[128]{0:T(128)} %param.6) | copy-start | bytes 1540

commit v2 on v0

v2 whole, which is shorter than its diff:
```python
import jax
import jax.numpy as jnp
from jax import lax
from jax.experimental import pallas as pl
from jax.experimental.pallas import tpu as pltpu
from jax.sharding import PartitionSpec as P

MESH = pl.DeviceIdType.MESH
OFF = (0, 768, 1536, 2304, 3328)
SIZE = (768, 768, 768, 1024, 768)
PIECES = 5
DEPTH = 4096
HALF = 64
ROWS = 128
COLS = 1024
STRIP = 32
STAGE = 256
BUFS = 4
SLOTS = 8

OWN = (0, 0)
FULL, TOP, LOW = (0, 64), (0, 32), (32, 32)


def slot_of(place):
    return place[0] * 4 + place[1]


NEAR = [(1, 0), (0, 1), (0, 3)]
ARRIVALS = [[(place, p, [FULL]) for place in NEAR] for p in range(PIECES)] + [
    [((0, 2), 0, [FULL]), ((0, 2), 1, [FULL]), ((1, 1), 3, [FULL])],
    [((0, 2), 2, [TOP, LOW]), ((1, 1), 0, [FULL])],
    [((1, 3), 3, [FULL]), ((0, 2), 3, [FULL]), ((0, 2), 4, [FULL])],
    [((1, 1), 4, [FULL]), ((1, 3), 0, [FULL])],
    [((1, 1), 1, [FULL]), ((1, 3), 4, [FULL]), ((1, 3), 1, [FULL])],
    [((1, 1), 2, [FULL]), ((1, 3), 2, [FULL])],
    [((1, 2), 3, [FULL]), ((1, 2), 0, [FULL])],
    [((1, 2), 1, [FULL]), ((1, 2), 4, [FULL]), ((1, 2), 2, [TOP, LOW])],
]
RELAYS = {
    0: [("z+", (0, 3), 0, FULL, (0, 2))],
    1: [("z-", (0, 1), 1, FULL, (0, 2))],
    2: [("z+", (0, 3), 2, TOP, (0, 2)), ("z-", (0, 1), 2, LOW, (0, 2)),
        ("z-", (1, 0), 0, FULL, (1, 1))],
    3: [("z+", (0, 3), 3, FULL, (0, 2)), ("z+", (1, 0), 0, FULL, (1, 3)),
        ("y", (0, 1), 3, FULL, (1, 1)), ("y", (0, 3), 3, FULL, (1, 3))],
    4: [("z-", (0, 1), 4, FULL, (0, 2)), ("z-", (1, 0), 1, FULL, (1, 1)),
        ("z-", (1, 0), 2, FULL, (1, 1)), ("z+", (1, 0), 1, FULL, (1, 3)),
        ("z+", (1, 0), 2, FULL, (1, 3)), ("y", (0, 1), 4, FULL, (1, 1)),
        ("y", (0, 3), 4, FULL, (1, 3))],
    6: [("z-", (1, 1), 0, FULL, (1, 2))],
    7: [("y", (0, 2), 3, FULL, (1, 2)), ("y", (0, 2), 4, FULL, (1, 2))],
    9: [("z+", (1, 3), 1, FULL, (1, 2))],
    10: [("z+", (1, 3), 2, TOP, (1, 2)), ("z-", (1, 1), 2, LOW, (1, 2))],
}
SUM_X = {3: [(0, 0)], 9: [(1, 0), (0, 1)], 10: [(0, 3)], 11: [(0, 2)]}
SUM_Y = {6: [(0, 0)], 11: [(1, 0), (0, 1), (0, 3)]}


def kernel(
    i_hbm, t_hbm, o_ref,
    got, thi, tlo, stage, part, rx, ry, st, ob, ihi, ilo,
    stage_sem, own_sem, send_sem, recv_sem, fwd_sem, sib_sem,
    xs_sem, xr_sem, ys_sem, yr_sem, os_sem, or_sem,
):
    vc, op = lax.axis_index("vc"), lax.axis_index("op")
    x, yh = vc // 2, vc % 2
    yl, z, core = op // 8, (op // 2) % 4, op % 2

    def at(x_, yh_, yl_, z_, core_):
        return {"vc": x_ * 2 + yh_, "op": yl_ * 8 + z_ * 2 + core_}

    to = {
        "z+": at(x, yh, yl, (z + 1) % 4, core),
        "z-": at(x, yh, yl, (z + 3) % 4, core),
        "y": at(x, yh, 1 - yl, z, core),
        "c": at(x, yh, yl, z, 1 - core),
    }
    opposite = at(x, 1 - yh, yl, z, core)

    def stage_copy(s):
        return pltpu.make_async_copy(
            t_hbm.at[pl.ds(s * STAGE, STAGE)],
            stage.at[s % BUFS],
            stage_sem.at[s % BUFS],
        )

    for s in range(BUFS):
        stage_copy(s).start()

    first = pl.multiple_of(core * HALF, HALF)

    def depth(piece):
        return pl.ds(OFF[piece], SIZE[piece])

    mine = [
        pltpu.make_async_copy(
            i_hbm.at[:, depth(p)], got.at[0, pl.ds(first, HALF), depth(p)], own_sem.at[p]
        )
        for p in range(PIECES)
    ]
    for copy in mine:
        copy.start()

    barrier = pltpu.get_barrier_semaphore()
    partners = list(to.values()) + [opposite]
    partners += [at((x + d) % 4, yh, yl, z, core) for d in (1, 2, 3)]
    for partner in partners:
        pl.semaphore_signal(barrier, inc=1, device_id=partner, device_id_type=MESH)
    pl.semaphore_wait(barrier, len(partners))

    started = []
    counts = {"send": 0, "fwd": 0}

    def window(place, piece, base, rows):
        start = pl.multiple_of(base + rows[0], 32)
        return got.at[slot_of(place), pl.ds(start, rows[1]), depth(piece)]

    def which(rows):
        return 1 if rows == LOW else 0

    def send(src, link, place, piece, rows):
        copy = pltpu.make_async_remote_copy(
            src_ref=src,
            dst_ref=window(place, piece, first, rows),
            send_sem=send_sem.at[counts["send"]],
            recv_sem=recv_sem.at[slot_of(place), piece, which(rows)],
            device_id=to[link],
            device_id_type=MESH,
        )
        counts["send"] += 1
        copy.start()
        started.append(copy)

    def forward(src, place, piece, rows):
        copy = pltpu.make_async_remote_copy(
            src_ref=src,
            dst_ref=window(place, piece, first, rows),
            send_sem=fwd_sem.at[counts["fwd"]],
            recv_sem=sib_sem.at[slot_of(place), piece, which(rows)],
            device_id=to["c"],
            device_id_type=MESH,
        )
        counts["fwd"] += 1
        copy.start()
        started.append(copy)

    def arrival(ref, sem):
        pltpu.make_async_remote_copy(
            src_ref=ref,
            dst_ref=ref,
            send_sem=send_sem.at[0],
            recv_sem=sem,
            device_id=to["c"],
            device_id_type=MESH,
        ).wait_recv()

    def arrived(sem, place, piece, base, rows):
        arrival(window(place, piece, base, rows), sem.at[slot_of(place), piece, which(rows)])

    for p in range(PIECES):
        src = i_hbm.at[:, depth(p)]
        send(src, "y", (1, 0), p, FULL)
        send(src, "z+", (0, 3), p, FULL)
        send(src, "z-", (0, 1), p, FULL)
        forward(src, OWN, p, FULL)

    def split_stage(s):
        stage_copy(s).wait()

        @pl.loop(0, STAGE // 64)
        def _(k):
            rows = pl.ds(pl.multiple_of(k * 64, 64), 64)
            into = pl.ds(pl.multiple_of(s * STAGE + k * 64, 64), 64)
            v = stage[s % BUFS, rows, :]
            h = v.astype(jnp.bfloat16)
            thi[into, :] = h
            tlo[into, :] = (v - h.astype(jnp.float32)).astype(jnp.bfloat16)

        if s + BUFS < DEPTH // STAGE:
            stage_copy(s + BUFS).start()

    def x_copy(slot, k):
        other = (x + k) % 4
        return pltpu.make_async_remote_copy(
            src_ref=part.at[slot, pl.ds(pl.multiple_of(other * STRIP, STRIP), STRIP)],
            dst_ref=rx.at[slot, k - 1],
            send_sem=xs_sem.at[slot, k - 1],
            recv_sem=xr_sem.at[slot, k - 1],
            device_id=at(other, yh, yl, z, core),
            device_id_type=MESH,
        )

    done = {}

    def unit(place, piece):
        slot, size = slot_of(place), SIZE[piece]
        fresh = slot not in done
        done[slot] = done.get(slot, 0) + 1
        a = got[slot, :, OFF[piece] : OFF[piece] + size]
        h = a.astype(jnp.bfloat16)
        ihi[:, :size] = h
        ilo[:, :size] = (a - h.astype(jnp.float32)).astype(jnp.bfloat16)
        high, low = ihi[:, :size], ilo[:, :size]
        for c in range(0, COLS, 256):
            t = thi[OFF[piece] : OFF[piece] + size, c : c + 256]
            r = jnp.dot(high, t, preferred_element_type=jnp.float32)
            r += jnp.dot(low, t, preferred_element_type=jnp.float32)
            t = tlo[OFF[piece] : OFF[piece] + size, c : c + 256]
            r += jnp.dot(high, t, preferred_element_type=jnp.float32)
            part[slot, :, c : c + 256] = r if fresh else part[slot, :, c : c + 256] + r
        if done[slot] == PIECES:
            for k in (2, 1, 3):
                x_copy(slot, k).start()

    strip = pl.ds(pl.multiple_of(x * STRIP, STRIP), STRIP)

    def block_owner(slot):
        row = (yl + slot // 4) % 2
        ring = (z + slot % 4) % 4
        return row * 2 + ring // 2, ring % 2

    def y_copy(slot):
        return pltpu.make_async_remote_copy(
            src_ref=st.at[slot],
            dst_ref=ry.at[slot],
            send_sem=ys_sem.at[slot],
            recv_sem=yr_sem.at[slot],
            device_id=opposite,
            device_id_type=MESH,
        )

    def o_copy(slot):
        ox, _ = block_owner(slot)
        k = (x + 3 - ox) % 4
        return pltpu.make_async_remote_copy(
            src_ref=st.at[slot],
            dst_ref=ob.at[strip],
            send_sem=os_sem.at[slot],
            recv_sem=or_sem.at[k],
            device_id=at(ox, yh, yl, z, core),
            device_id_type=MESH,
        )

    def sum_x(place):
        slot = slot_of(place)
        for k in range(3):
            arrival(rx.at[slot, k], xr_sem.at[slot, k])
        st[slot] = (part[slot, strip, :] + rx[slot, 0]) + (rx[slot, 1] + rx[slot, 2])

        @pl.when(block_owner(slot)[1] != yh)
        def _():
            y_copy(slot).start()

    def sum_y(place):
        slot = slot_of(place)
        ox, oyh = block_owner(slot)

        @pl.when(oyh == yh)
        def _():
            arrival(ry.at[slot], yr_sem.at[slot])
            st[slot] = st[slot] + ry[slot]

            @pl.when(ox == x)
            def _():
                ob[strip, :] = st[slot]

            @pl.when(ox != x)
            def _():
                o_copy(slot).start()

    ready = 0
    for p in range(PIECES):
        while ready * STAGE < OFF[p] + SIZE[p]:
            split_stage(ready)
            ready += 1
        mine[p].wait()
        arrived(sib_sem, OWN, p, HALF - first, FULL)
        unit(OWN, p)

    for number, group in enumerate(ARRIVALS):
        for place, piece, ranges in group:
            for rows in ranges:
                arrived(recv_sem, place, piece, first, rows)
                forward(window(place, piece, first, rows), place, piece, rows)
        for link, place, piece, rows, there in RELAYS.get(number, []):
            send(window(place, piece, first, rows), link, there, piece, rows)
        for place, piece, ranges in group:
            for rows in ranges:
                arrived(sib_sem, place, piece, HALF - first, rows)
            unit(place, piece)
        for place in SUM_X.get(number, []):
            sum_x(place)
        for place in SUM_Y.get(number, []):
            sum_y(place)

    sum_x((1, 1))
    sum_x((1, 3))
    sum_y((0, 2))
    sum_x((1, 2))
    sum_y((1, 1))
    sum_y((1, 3))
    sum_y((1, 2))

    for k in range(3):
        other = pl.multiple_of((x + 1 + k) % 4 * STRIP, STRIP)
        arrival(ob.at[pl.ds(other, STRIP)], or_sem.at[k])
    o_ref[...] = ob[...]

    for copy in started:
        copy.wait_send()
    for slot in range(SLOTS):
        for k in (1, 2, 3):
            x_copy(slot, k).wait_send()
        ox, oyh = block_owner(slot)

        @pl.when(oyh != yh)
        def _():
            y_copy(slot).wait_send()

        @pl.when((oyh == yh) & (ox != x))
        def _():
            o_copy(slot).wait_send()


def shards(integrals, amplitudes, vir_energy, occ_energy):
    f32, bf16, dma = jnp.float32, jnp.bfloat16, pltpu.SemaphoreType.DMA
    ladder = pl.pallas_call(
        kernel,
        out_shape=jax.ShapeDtypeStruct((ROWS, COLS), f32),
        in_specs=[pl.BlockSpec(memory_space=pl.ANY)] * 2,
        out_specs=pl.BlockSpec(memory_space=pltpu.VMEM),
        scratch_shapes=[
            pltpu.VMEM((SLOTS, ROWS, DEPTH), f32),
            pltpu.VMEM((DEPTH, COLS), bf16),
            pltpu.VMEM((DEPTH, COLS), bf16),
            pltpu.VMEM((BUFS, STAGE, COLS), f32),
            pltpu.VMEM((SLOTS, ROWS, COLS), f32),
            pltpu.VMEM((SLOTS, 3, STRIP, COLS), f32),
            pltpu.VMEM((SLOTS, STRIP, COLS), f32),
            pltpu.VMEM((SLOTS, STRIP, COLS), f32),
            pltpu.VMEM((ROWS, COLS), f32),
            pltpu.VMEM((ROWS, 1024), bf16),
            pltpu.VMEM((ROWS, 1024), bf16),
            dma((BUFS,)),
            dma((PIECES,)),
            dma((40,)),
            dma((SLOTS, PIECES, 2)),
            dma((48,)),
            dma((SLOTS, PIECES, 2)),
            dma((SLOTS, 3)),
            dma((SLOTS, 3)),
            dma((SLOTS,)),
            dma((SLOTS,)),
            dma((SLOTS,)),
            dma((3,)),
        ],
        compiler_params=pltpu.CompilerParams(
            collective_id=0, has_side_effects=True, vmem_limit_bytes=60 << 20
        ),
        name="ladder",
    )(integrals, amplitudes)
    return ladder / (occ_energy[None, :] - vir_energy[:, None])


def solution(mesh):
    return jax.shard_map(
        shards,
        mesh=mesh,
        in_specs=(P("op", "vc"), P("vc", "op"), P("vc"), P("op")),
        out_specs=P("vc", "op"),
        check_vma=False,
    )
```

time: 236 us -> 101 us (0.43)
  waiting for transfers between devices: 153 us -> 0 us
  Pallas kernels: 0 us -> 98.5 us
  matrix products: 61.4 us -> 0 us
  between operations: 13.2 us -> 0.03 us
  other arithmetic: 4.47 us -> 1.98 us
    pallas_call x0 -> x1, Pallas kernels: none -> 98.5 us  [shards(): pl.pallas_call(kernel, out_shape=jax.ShapeDtypeStruct((ROWS, COLS), f32),...]
    all_gather x2 -> x0, waiting for transfers between devices: 78.1 us -> none  [work_in_pieces(): blocks = [lax.all_gather(piece, axis) for piece in pieces]]
    reduce_scatter x2 -> x0, waiting for transfers between devices: 74.3 us -> none  [sum_by_axis(): nearer = lax.psum_scatter(shard, axes[0], scatter_dimension=dim, tiled=True)]
    dot_general x2 -> x0, matrix products: 61.4 us -> none  [product(): jnp.dot(piece, amplitudes, precision=lax.Precision.HIGHEST, preferred_ele...]
    concatenate x1 -> x0, other arithmetic: 2.49 us -> none  [work_in_pieces(): return in_order(jnp.concatenate(made, axis=out_dim + 1), out_dim)]
  transfers between devices with their start and end apart: 4 -> 0, of which waited for: 4 -> 0; matrix products, arithmetic and copies ran while one was open for 13% -> 0% of each run, Pallas kernels for 0% -> 0%
where the time goes in v2:
time: 101 us
  Pallas kernels  98.5 us (98%)
  other arithmetic  1.98 us (2%)
    pallas_call x1, Pallas kernels, shards(): pl.pallas_call(kernel, out_shape=jax.ShapeDtypeStruct((ROWS, COLS), f32),...  98.5 us

profile of v2, /device:TPU:6, one launch (start us, length us, event | category | flops | bytes accessed | tf_op | source)
XLA Modules:
  0.0 100.5 jit_solution(11482017014833636652)
XLA Ops:
  0.0 0.0 copy-start
  0.0 0.0 copy-start.1
  0.0 98.5 %ladder.1 = f32[128,1024]{1,0:T(8,128)} custom-call(f32[64,4096]{1,0:T(8,128)} %i_hbm.1, f32[4096,1024]{1,0:T(8,128)} %t_hbm.1), custom_call_target="tpu_custom_call" | custom-call | tf_op jit(solution)/shard_map/ladder/pallas_call | solution.py:328
  98.5 0.0 copy-done
  98.6 0.0 copy-done.1
  98.6 2.0 %subtract_divide_fusion = f32[128,1024]{1,0:T(8,128)} fusion(f32[128,1024]{1,0:T(8,128)} %ladder.1, f32[128]{0:T(128)S(1)} %copy-done.1, f32[1024]{0:T(1024)S(1)} %copy-done), kind=kLoop, calls=%fused_computation | loop fusion | flops 262144 | bytes 1053184 | tf_op jit(solution)/shard_map/div | solution.py:363
Async XLA Ops:
  0.0 98.5 %copy-start = (f32[1024]{0:T(1024)S(1)}, f32[1024]{0:T(1024)}, u32[]{:S(2)}) copy-start(f32[1024]{0:T(1024)} %param.7) | copy-start | bytes 12292
  0.0 98.6 %copy-start.1 = (f32[128]{0:T(128)S(1)}, f32[128]{0:T(128)}, u32[]{:S(2)}) copy-start(f32[128]{0:T(128)} %param.6) | copy-start | bytes 1540
